TPU v7x, 512 devices: a whole 4x8x8 slice. The times are simulated.
512 devices in a mesh: grp: 16 (over y, x_hi), blk: 32 (over x_lo, z, core).
Axes of the slice: x: 4 (x_hi: 2, x_lo: 2; x = x_hi * 2 + x_lo), y: 8, z: 8, core: 2. Of those that a mesh axis runs over, the one named last changes fastest.
Arguments:
- sigma_anc: float32 [16384, 16384], P('grp', 'blk')
- panels: float32 [16384, 1024], P(('grp', 'blk')), may hold values from -0.0625 to 0.0625
- diag_inv: float32 [1024, 256], replicated, may hold values from -6 to 6
- scaled_parent_panel: float32 [512, 256], replicated, may hold values from -0.375 to 0.375
- struct_upper: int32 [2, 32], replicated, may hold values from 0 to 63, as said below
- struct_lower: int32 [2, 16], replicated, may hold values from 0 to 63, as said below
Outputs:
- cov_panel: float32 [16384, 1024], P(('blk', 'grp'))
- cov_diag: float32 [1024, 256], P('blk')
- cov_parent: float32 [512, 256], P('blk')
Inputs may be any that keep to these rules, and one draw needn't show every extreme that they name: `struct_upper`: each row lists 32 different ancestor blocks. `struct_lower`: each row lists 16 different blocks, all in its parent's row of struct_upper.
All inputs are finite; a program needn't handle non-finite values.
Results may differ from a plain program's by a relative error of at most 0.00011.
Values sent between devices are 32-bit elements; how exact they have to be, the bound alone decides.
A program may use at most 64 MiB of HBM per device.

v0:
```python
import jax
import jax.numpy as jnp
from jax import lax
from jax.sharding import PartitionSpec as P

NODE_WIDTH = 256
UPPER_NODES_1 = 2
LOWER_NODES_2 = 2
HIGH_ACCURACY = lax.Precision.HIGHEST


def block_table(struct_upper, struct_lower, blocks):
    ids = jnp.arange(blocks, dtype=jnp.int32)
    upper = jnp.any(struct_upper[:, :, None] == ids[None, None, :], axis=1)
    lower = jnp.any(struct_lower[:, :, None] == ids[None, None, :], axis=1)
    return jnp.concatenate([upper, lower], axis=0).astype(jnp.float32)


def row_mask(table, first_row, count):
    blocks = table.shape[1]
    rows = first_row + jnp.arange(count, dtype=jnp.int32)
    membership_grid = (
        (rows // NODE_WIDTH)[:, None] == jnp.arange(blocks, dtype=jnp.int32)[None, :]
    ).astype(jnp.float32)
    return jnp.dot(
        membership_grid, table.T, precision=HIGH_ACCURACY, preferred_element_type=jnp.float32
    )


def strip_summands(reciprocal_lines, array_lines, membership_grid, stacked_arrays):
    count = reciprocal_lines.shape[0]
    upper_width_1 = UPPER_NODES_1 * NODE_WIDTH
    matrix_columns = jnp.repeat(array_lines, NODE_WIDTH, axis=1)
    g_up = -(matrix_columns[:, :upper_width_1] * reciprocal_lines[:, :upper_width_1])
    collected_elder_share = jnp.einsum(
        "rjw,cj->rcw",
        g_up.reshape(count, UPPER_NODES_1, NODE_WIDTH),
        membership_grid,
        precision=HIGH_ACCURACY,
    )
    resolved_bottom_share = matrix_columns[:, upper_width_1:].reshape(
        count, LOWER_NODES_2, NODE_WIDTH
    ) * (
        jnp.einsum("odf,dfy->ody", collected_elder_share, stacked_arrays, precision=HIGH_ACCURACY)
        + reciprocal_lines[:, upper_width_1:].reshape(count, LOWER_NODES_2, NODE_WIDTH)
    )
    strip_result = jnp.concatenate(
        [g_up, -resolved_bottom_share.reshape(count, LOWER_NODES_2 * NODE_WIDTH)], axis=1
    )
    return (strip_result, collected_elder_share, resolved_bottom_share)


def block_sums(urows, reciprocal_lines, collected_elder_share, resolved_bottom_share):
    count = urows.shape[0]
    upper_width_1 = UPPER_NODES_1 * NODE_WIDTH
    u_up = urows[:, :upper_width_1].reshape(count, UPPER_NODES_1, NODE_WIDTH)
    u_low = urows[:, upper_width_1:].reshape(count, LOWER_NODES_2, NODE_WIDTH)
    amat = jnp.einsum(
        "rjw,rjv->jwv",
        u_up,
        reciprocal_lines[:, :upper_width_1].reshape(count, UPPER_NODES_1, NODE_WIDTH),
        precision=HIGH_ACCURACY,
    )
    block_matrix = jnp.einsum("rcw,rcv->cwv", u_low, collected_elder_share, precision=HIGH_ACCURACY)
    extra_matrix = jnp.einsum("rcw,rcv->cwv", u_low, resolved_bottom_share, precision=HIGH_ACCURACY)
    return jnp.concatenate([amat, block_matrix, extra_matrix], axis=0)


def per_device(sigma_anc, panels, diag_inv, scaled_parent_panel, struct_upper, struct_lower):
    rows_grp, cols_dev = sigma_anc.shape
    rows_dev = panels.shape[0]
    grp_count = lax.axis_size("grp")
    blk_count = lax.axis_size("blk")
    grp_pos = lax.axis_index("grp")
    blk_pos = lax.axis_index("blk")
    blocks = cols_dev * blk_count // NODE_WIDTH
    table = block_table(struct_upper, struct_lower, blocks)
    parent_ids = jnp.arange(LOWER_NODES_2, dtype=jnp.int32) % UPPER_NODES_1
    membership_grid = (
        parent_ids[:, None] == jnp.arange(UPPER_NODES_1, dtype=jnp.int32)[None, :]
    ).astype(jnp.float32)
    stacked_arrays = scaled_parent_panel.reshape(LOWER_NODES_2, NODE_WIDTH, NODE_WIDTH)
    first_in = grp_pos * rows_grp + blk_pos * rows_dev
    upanel = panels * jnp.repeat(row_mask(table, first_in, rows_dev), NODE_WIDTH, axis=1)
    grouped = lax.all_gather(upanel, "blk", axis=0, tiled=True)
    partial_value = lax.dot_general(
        sigma_anc,
        grouped,
        (((0,), (0,)), ((), ())),
        precision=HIGH_ACCURACY,
        preferred_element_type=jnp.float32,
    )
    share = cols_dev // grp_count
    col_first = blk_pos * cols_dev
    root = col_first // rows_grp
    offset = jnp.clip(col_first - grp_pos * rows_grp, 0, rows_grp - cols_dev)
    own_first = col_first + grp_pos * share
    owned_mask = row_mask(table, own_first, share)
    nterms = UPPER_NODES_1 + 2 * LOWER_NODES_2
    inverse_columns = lax.psum(partial_value, "grp")
    inverse_owned = lax.dynamic_slice_in_dim(inverse_columns, grp_pos * share, share, 0)
    strip_result, collected_elder_share, resolved_bottom_share = strip_summands(
        inverse_owned, owned_mask, membership_grid, stacked_arrays
    )

    def on_root():
        u_cols = lax.dynamic_slice_in_dim(grouped, offset, cols_dev, 0)
        complete_mask = row_mask(table, col_first, cols_dev)
        discarded_result, collected_entire_factor, resolved_entire_factor = strip_summands(
            inverse_columns, complete_mask, membership_grid, stacked_arrays
        )
        return block_sums(u_cols, inverse_columns, collected_entire_factor, resolved_entire_factor)

    def off_root():
        return jnp.zeros((nterms, NODE_WIDTH, NODE_WIDTH), jnp.float32)

    terms = lax.cond(grp_pos == root, on_root, off_root)
    summed = lax.psum(terms, ("grp", "blk"))
    amat = summed[:UPPER_NODES_1]
    block_matrix = summed[UPPER_NODES_1 : UPPER_NODES_1 + LOWER_NODES_2]
    extra_matrix = summed[UPPER_NODES_1 + LOWER_NODES_2 :]
    diagonal_matrices = diag_inv.reshape(UPPER_NODES_1 + LOWER_NODES_2, NODE_WIDTH, NODE_WIDTH)
    s_up = diagonal_matrices[:UPPER_NODES_1] + amat
    parent_selection = jnp.einsum("cj,jwv->cwv", membership_grid, s_up, precision=HIGH_ACCURACY)
    solved_parent = jnp.einsum(
        "ghz,gzs->ghs", parent_selection, stacked_arrays, precision=HIGH_ACCURACY
    ) + jnp.transpose(block_matrix, (0, 2, 1))
    lower_selection = (
        diagonal_matrices[UPPER_NODES_1:]
        + jnp.einsum("lmt,lmx->ltx", stacked_arrays, solved_parent, precision=HIGH_ACCURACY)
        + extra_matrix
    )
    whole_diag = jnp.concatenate([s_up, lower_selection], axis=0).reshape(
        (UPPER_NODES_1 + LOWER_NODES_2) * NODE_WIDTH, NODE_WIDTH
    )
    whole_parent = -solved_parent.reshape(LOWER_NODES_2 * NODE_WIDTH, NODE_WIDTH)
    diag_rows = (UPPER_NODES_1 + LOWER_NODES_2) * NODE_WIDTH // blk_count
    parent_rows = LOWER_NODES_2 * NODE_WIDTH // blk_count
    cov_diag = lax.dynamic_slice_in_dim(whole_diag, blk_pos * diag_rows, diag_rows, 0)
    cov_parent = lax.dynamic_slice_in_dim(whole_parent, blk_pos * parent_rows, parent_rows, 0)
    return (strip_result, cov_diag, cov_parent)


def solution(mesh):
    return jax.shard_map(
        per_device,
        mesh=mesh,
        in_specs=(P("grp", "blk"), P(("grp", "blk"), None), P(), P(), P(), P()),
        out_specs=(P(("blk", "grp"), None), P("blk", None), P("blk", None)),
        check_vma=False,
    )
```

profile of v0, /device:TPU:17, one launch (start us, length us, event | category | flops | bytes accessed | tf_op | source)
XLA Modules:
  0.0 598.6 jit_solution(4750005704873806624)
XLA Ops:
  7.2 0.0 copy-start
  7.2 0.0 all-gather.2.cloned.1.call-start
  7.3 0.9 fusion.21
  8.2 0.8 fusion.22
  8.9 0.2 fusion.23
  9.1 0.1 broadcast_in_dim.7
  9.3 1.6 mul.37
  10.8 0.0 all-gather.2.cloned.1.call-update
  10.9 0.0 all-reduce.3.cloned.1.call-start
  10.9 74.6 %all-gather.2.cloned.1.call-done = f32[1024,1024]{1,0:T(8,128)} async-done(((f32[32,1024]{1,0:T(8,128)}), f32[1024,1024]{1,0:T(8,128)}) %all-gather.2.cloned.1.call-update) | async-done | bytes 4194320 | tf_op jit(solution)/shard_map/all_gather | solution.py:85
  85.5 0.0 copy-done
  85.5 9.6 %convolution_bitcast_fusion.2 = f32[512,1024]{0,1:T(8,128)} fusion(f32[1024,1024]{1,0:T(8,128)} %all-gather.2.cloned.1.call-done, f32[1024,512]{1,0:T(8,128)S(1)} %copy-done), kind=kOutput, calls=%fused_computation.24 | convolution fusion | flops 6442450944 | bytes 8388608 | tf_op jit(solution)/shard_map/dot_general | solution.py:86
  95.1 0.0 copy-start.8
  95.1 0.0 all-reduce.3.cloned.1.call-update
  95.2 0.0 all-reduce.5.cloned.1.call-start
  95.3 0.1 fusion.30
  95.3 1.0 copy-done.8
  96.4 1.1 fusion.35
  97.5 157.6 %all-reduce.3.cloned.1.call-done = f32[512,1024]{0,1:T(8,128)} async-done(((f32[512,1024]{0,1:T(8,128)}), f32[512,1024]{0,1:T(8,128)}) %all-reduce.3.cloned.1.call-update) | async-done | bytes 2097168 | tf_op jit(solution)/shard_map/psum | solution.py:100
  255.0 1.3 conditional.1
  255.0 1.3 broadcast.130
  256.4 0.0 copy-start.7
  256.4 3.1 copy.93
  259.4 0.0 copy-start.6
  259.4 0.0 all-reduce.5.cloned.1.call-update
  259.5 0.2 fusion.24
  259.7 0.0 copy-done.7
  259.7 1.0 copy.94
  260.7 0.0 copy-done.6
  260.7 1.0 copy.99
  261.7 0.0 copy-start.1
  261.7 1.3 fusion.19
  263.0 0.1 copy.91
  263.1 0.1 copy.86
  263.3 0.1 copy.88
  263.4 0.1 copy.89
  263.5 0.3 convolution_bitcast_fusion.4
  263.8 0.0 copy-done.1
  263.8 0.4 fusion.17
  264.2 0.7 pad_maximum_fusion.2
  264.9 313.5 %all-reduce.5.cloned.1.call-done = f32[6,256,256]{1,2,0:T(8,128)} async-done(((f32[6,256,256]{1,2,0:T(8,128)}), f32[6,256,256]{1,2,0:T(8,128)}) %all-reduce.5.cloned.1.call-update) | async-done | bytes 1572880 | tf_op jit(solution)/shard_map/psum | solution.py:118
  578.4 1.3 slice_add_fusion
  579.7 1.0 copy.95
  580.7 0.0 copy-start.5
  580.7 2.2 fusion.27
  582.9 2.5 fusion.36
  585.4 0.0 copy-done.5
  585.4 2.1 fusion.13
  587.5 1.0 pad_maximum_fusion.1
  588.5 1.6 copy.100
  590.1 0.6 constant_dynamic-slice_fusion.2
  590.7 1.3 constant_dynamic-slice_fusion.1
  (7 shorter events, 0.1 us)
Async XLA Ops:
  7.2 78.4 %copy-start = (f32[1024,512]{1,0:T(8,128)S(1)}, f32[1024,512]{1,0:T(8,128)}, u32[]{:S(2)}) copy-start(f32[1024,512]{1,0:T(8,128)} %param.8) | copy-start | bytes 6291460
  7.2 78.3 %all-gather.2.cloned.1.call-start = ((), (), s32[]{:S(2)}) async-start(), calls=%async_computation | async-start | bytes 4325376 | tf_op jit(solution)/shard_map/all_gather | solution.py:85
  10.9 244.2 %all-reduce.3.cloned.1.call-start = ((), (), s32[]{:S(2)}) async-start(), calls=%async_computation.1 | async-start | bytes 4194304 | tf_op jit(solution)/shard_map/psum | solution.py:100
  95.1 1.2 copy-start.8
  95.2 483.3 %all-reduce.5.cloned.1.call-start = ((), (), s32[]{:S(2)}) async-start(), calls=%async_computation.2 | async-start | bytes 3145728 | tf_op jit(solution)/shard_map/psum | solution.py:118
  256.4 3.3 copy-start.7
  259.4 1.2 copy-start.6
  261.7 2.1 copy-start.1
  580.7 4.7 copy-start.5
Sparse Core Ops, SparseCore 0:
  11.0 74.4 all-gather.1
  95.3 159.7 all-reduce.2
  259.9 318.4 all-reduce.4
where the time goes:
time: 599 us
  waiting for transfers between devices  546 us (91%)
  matrix products  17.5 us (3%)
  between operations  13.9 us (2%)
  local copies, waits for them, and re-layouts  13.7 us (2%)
  other arithmetic  7.63 us (1%)
    psum x1, waiting for transfers between devices, per_device(): summed = lax.psum(terms, ('grp', 'blk'))  314 us
    psum x1, waiting for transfers between devices, per_device(): inverse_columns = lax.psum(partial_value, 'grp')  158 us
    all_gather x1, waiting for transfers between devices, per_device(): grouped = lax.all_gather(upanel, 'blk', axis=0, tiled=True)  74.6 us
  transfers between devices with their start and end apart: 3, of which 3 were waited for; matrix products, arithmetic and copies ran while one was open for 1% of the time, Pallas kernels for 0%

commit v1 on v0

--- a/solution.py
+++ b/solution.py
@@ -82,7 +82,9 @@
     stacked_arrays = scaled_parent_panel.reshape(LOWER_NODES_2, NODE_WIDTH, NODE_WIDTH)
     first_in = grp_pos * rows_grp + blk_pos * rows_dev
     upanel = panels * jnp.repeat(row_mask(table, first_in, rows_dev), NODE_WIDTH, axis=1)
-    grouped = lax.all_gather(upanel, "blk", axis=0, tiled=True)
+    grouped = jnp.concatenate(
+        lax.all_to_all(jnp.stack([upanel] * lax.axis_size("blk")), "blk", 0, 0), axis=0
+    )
     partial_value = lax.dot_general(
         sigma_anc,
         grouped,

time: 599 us -> 631 us (1.053)
  blocking collectives: 0 us -> 106 us
  waiting for transfers between devices: 546 us -> 471 us
    all_to_all x0 -> x1, blocking collectives: none -> 106 us  [per_device(): lax.all_to_all(jnp.stack([upanel] * lax.axis_size('blk')), 'blk', 0, 0)]
    all_gather x1 -> x0, waiting for transfers between devices: 74.6 us -> none  [per_device(): grouped = lax.all_gather(upanel, 'blk', axis=0, tiled=True)]
  transfers between devices with their start and end apart: 3 -> 2, of which waited for: 3 -> 2; matrix products, arithmetic and copies ran while one was open for 1% -> 1% of each run, Pallas kernels for 0% -> 0%
where the time goes in v1:
time: 631 us; the launch traced here: 630 us
  waiting for transfers between devices  471 us (75%)
  blocking collectives  106 us (17%)
  local copies, waits for them, and re-layouts  16.1 us (3%)
  matrix products  16 us (3%)
  between operations  14.2 us (2%)
  other arithmetic  6.97 us (1%)
    psum x1, waiting for transfers between devices, per_device(): summed = lax.psum(terms, ('grp', 'blk'))  313 us
    psum x1, waiting for transfers between devices, per_device(): inverse_columns = lax.psum(partial_value, 'grp')  157 us
    all_to_all x1, blocking collectives, per_device(): lax.all_to_all(jnp.stack([upanel] * lax.axis_size('blk')), 'blk', 0, 0)  106 us
  transfers between devices with their start and end apart: 2, of which 2 were waited for; matrix products, arithmetic and copies ran while one was open for 1% of the time, Pallas kernels for 0%

profile of v1, /device:TPU:17, one launch (start us, length us, event | category | flops | bytes accessed | tf_op | source)
XLA Modules:
  0.0 630.0 jit_solution(12287573798359658634)
XLA Ops:
  7.2 0.0 copy-start
  7.2 0.0 all-reduce.3.cloned.1.call-start
  7.3 0.9 fusion.21
  8.2 0.8 fusion.22
  8.9 0.2 fusion.23
  9.1 0.1 broadcast_in_dim.7
  9.3 0.9 mul.37
  10.2 0.5 stack.2
  10.7 105.8 %all_to_all.5 = f32[32,32,1024]{2,1,0:T(8,128)S(1)} all-to-all(f32[32,32,1024]{2,1,0:T(8,128)S(1)} %stack.2), channel_id=1, replica_groups=mesh['grp'=16,'blk'=32] {'blk'}, dimensions={0} | all-to-all | bytes 8388608 | tf_op jit(solution)/shard_map/all_to_all | solution.py:86
  116.5 0.0 copy-start.1
  116.5 2.0 copy-done.1
  118.5 0.0 copy-done
  118.5 8.1 %convolution_bitcast_fusion.2 = f32[512,1024]{0,1:T(8,128)} fusion(f32[1024,1024]{1,0:T(8,128)S(1)} %bitcast.78, f32[1024,512]{1,0:T(8,128)S(1)} %copy-done), kind=kOutput, calls=%fused_computation.24 | convolution fusion | flops 6442450944 | bytes 8388608 | tf_op jit(solution)/shard_map/dot_general | solution.py:88
  126.6 0.0 copy-start.9
  126.6 0.0 all-reduce.3.cloned.1.call-update
  126.6 0.0 all-reduce.5.cloned.1.call-start
  126.7 0.1 fusion.30
  126.8 1.0 copy-done.9
  127.8 1.1 fusion.35
  128.9 157.3 %all-reduce.3.cloned.1.call-done = f32[512,1024]{0,1:T(8,128)} async-done(((f32[512,1024]{0,1:T(8,128)}), f32[512,1024]{0,1:T(8,128)}) %all-reduce.3.cloned.1.call-update) | async-done | bytes 2097168 | tf_op jit(solution)/shard_map/psum | solution.py:102
  286.2 1.3 conditional.1
  286.2 1.3 broadcast.132
  287.5 0.0 copy-start.8
  287.5 3.1 copy.95
  290.6 0.0 copy-start.7
  290.6 0.0 all-reduce.5.cloned.1.call-update
  290.7 0.2 fusion.24
  290.8 0.0 copy-done.8
  290.8 1.0 copy.96
  291.9 0.0 copy-done.7
  291.9 1.0 copy.101
  292.9 0.0 copy-start.2
  292.9 1.3 fusion.19
  294.2 0.1 copy.93
  294.3 0.1 copy.88
  294.4 0.1 copy.90
  294.6 0.1 copy.91
  294.7 0.3 convolution_bitcast_fusion.4
  295.0 0.0 copy-done.2
  295.0 0.4 fusion.17
  295.4 0.7 pad_maximum_fusion.2
  296.1 313.5 %all-reduce.5.cloned.1.call-done = f32[6,256,256]{1,2,0:T(8,128)} async-done(((f32[6,256,256]{1,2,0:T(8,128)}), f32[6,256,256]{1,2,0:T(8,128)}) %all-reduce.5.cloned.1.call-update) | async-done | bytes 1572880 | tf_op jit(solution)/shard_map/psum | solution.py:120
  609.6 1.3 slice_add_fusion
  610.8 1.0 copy.97
  611.8 0.0 copy-start.6
  611.8 2.2 fusion.27
  614.0 2.5 fusion.36
  616.5 0.0 copy-done.6
  616.5 2.1 fusion.13
  618.6 1.0 pad_maximum_fusion.1
  619.7 1.6 copy.102
  621.2 0.6 constant_dynamic-slice_fusion.2
  621.8 1.3 constant_dynamic-slice_fusion.1
  (7 shorter events, 0.1 us)
Async XLA Ops:
  7.2 111.3 %copy-start = (f32[1024,512]{1,0:T(8,128)S(1)}, f32[1024,512]{1,0:T(8,128)}, u32[]{:S(2)}) copy-start(f32[1024,512]{1,0:T(8,128)} %param.8) | copy-start | bytes 6291460
  7.2 279.0 %all-reduce.3.cloned.1.call-start = ((), (), s32[]{:S(2)}) async-start(), calls=%async_computation.1 | async-start | bytes 4194304 | tf_op jit(solution)/shard_map/psum | solution.py:102
  116.5 2.0 copy-start.1
  126.6 1.2 copy-start.9
  126.6 483.0 %all-reduce.5.cloned.1.call-start = ((), (), s32[]{:S(2)}) async-start(), calls=%async_computation.2 | async-start | bytes 3145728 | tf_op jit(solution)/shard_map/psum | solution.py:120
  287.5 3.3 copy-start.8
  290.6 1.2 copy-start.7
  292.9 2.1 copy-start.2
  611.8 4.7 copy-start.6
Sparse Core Ops, SparseCore 0:
  126.7 159.4 all-reduce.2
  291.1 318.3 all-reduce.4
